TPU v7x, 32 devices: a whole 2x2x4 slice. The times are simulated.
32 devices in a mesh: row: 4 (over y, core), col: 8 (over z, x).
Axes of the slice: x: 2, y: 2, z: 4, core: 2. Of those that a mesh axis runs over, the one named last changes fastest.
Arguments:
- kernels: bfloat16 [6, 4096, 6144], P(None, 'col', 'row'), may hold values from -0.03125 to 0.03125
- history: bfloat16 [6, 6144, 256], P(None, ('row', 'col')), may hold values from -6 to 6
- incident: float32 [32, 128, 256], P(('row', 'col')), may hold values from -6 to 6
- owner: int32 [32], replicated, may hold values from 0 to 3, as said below
- tile_pairs: int32 [384, 2], P(('row', 'col')), may hold values from 0 to 31, as said below
- tile_values: bfloat16 [384, 128, 128], P(('row', 'col')), may hold values from -0.109375 to 0.109375
- tile_counts: int32 [32], P(('row', 'col')), may hold values from 1 to 12, as said below
Outputs:
- density: float32 [32, 128, 256], P(('row', 'col'))
Inputs may be any that keep to these rules, and one draw needn't show every extreme that they name: `owner`: within each block of 4 consecutive clusters starting at a multiple of 4, the owners are all different. tile_pairs[t, 0] is the cluster whose slot is t // 12; for a target cluster k the sources of its slot are distinct clusters whose block (cluster // 4) is k // 4 - 1, k // 4 or k // 4 + 1, modulo 8. `tile_counts`: some device has all 12 slots live.
All inputs are finite; a program needn't handle non-finite values.
Results may differ from a plain program's by a relative error of at most 0.0012.
Values may be sent and summed in bfloat16 or wider, within the bound.
No kernel may reach another device: no remote copies, remote signals or barrier semaphores. Data moves between devices by JAX's collectives and lax.ppermute only.
A program may use at most 128 MiB of HBM per device.

v0:
```python
import jax
import jax.numpy as jnp
from jax import lax
from jax.sharding import PartitionSpec as P

SWEEPS = 3
damping = 0.7


def with_halo(cells, sides, width):
    for axis, dim in sides:
        count = lax.axis_size(axis)
        head = lax.slice_in_dim(cells, 0, width, axis=dim)
        tail = lax.slice_in_dim(cells, cells.shape[dim] - width, cells.shape[dim], axis=dim)
        cells = jnp.concatenate(
            [
                lax.ppermute(tail, axis, [(i, (i + 1) % count) for i in range(count)]),
                cells,
                lax.ppermute(head, axis, [((i + 1) % count, i) for i in range(count)]),
            ],
            axis=dim,
        )
    return cells


def per_device(kernels, history, incident, owner, tile_pairs, tile_values, tile_counts):
    row_count = lax.axis_size("row")
    col_count = lax.axis_size("col")
    columns = history.shape[2]
    cluster = incident.shape[1]
    retarded = lax.dot_general(
        kernels,
        lax.all_gather(history, "col", axis=1, tiled=True),
        (((0, 2), (0, 1)), ((), ())),
        preferred_element_type=jnp.float32,
    )
    col_index = lax.axis_index("col")
    row_index = lax.axis_index("row")
    block_owner = lax.dynamic_slice_in_dim(owner, col_index * row_count, row_count)
    positions = jnp.arange(row_count, dtype=jnp.int32)
    blocks = retarded.reshape(row_count, cluster, columns)
    block_sum = lax.psum_scatter(blocks, "row", scatter_dimension=0, tiled=True)
    everyone = lax.all_gather(block_sum, "row", axis=0, tiled=True)
    chosen = jnp.sum(jnp.where(block_owner == row_index, positions, 0))
    owned_sum = lax.dynamic_index_in_dim(everyone, chosen, 0, keepdims=False)
    driven = incident[0] - owned_sum
    sources = tile_pairs[:, 1]
    clusters = jnp.arange(owner.shape[0], dtype=jnp.int32)
    src_owner = jnp.sum(jnp.where(sources[:, None] == clusters[None, :], owner[None, :], 0), axis=1)
    src_block = sources // row_count
    window_slot = (src_block - col_index + 1 + col_count) % col_count * row_count + src_owner
    active = jnp.arange(tile_values.shape[0], dtype=jnp.int32) < tile_counts[0]
    density = driven
    for sweep_step in range(SWEEPS):
        rounded = density.astype(jnp.bfloat16)
        block_part = lax.all_gather(rounded, "row", axis=0, tiled=True)
        window = with_halo(block_part, (("col", 0),), row_count * cluster)
        window = window.reshape(-1, cluster, columns)
        picked = jnp.take(window, window_slot, axis=0)
        picked = jnp.where(active[:, None, None], picked, jnp.zeros((), jnp.bfloat16))
        near_term = lax.dot_general(
            tile_values, picked, (((0, 2), (0, 1)), ((), ())), preferred_element_type=jnp.float32
        )
        density = density + damping * (driven - density - near_term)
    return density[None]


def solution(mesh):
    in_specs = (
        P(None, "col", "row"),
        P(None, ("row", "col"), None),
        P(("row", "col"), None, None),
        P(),
        P(("row", "col"), None),
        P(("row", "col"), None, None),
        P(("row", "col")),
    )
    out_specs = P(("row", "col"), None, None)
    return jax.shard_map(
        per_device, mesh=mesh, in_specs=in_specs, out_specs=out_specs, check_vma=False
    )
```

profile of v0, /device:TPU:0, one launch (start us, length us, event | category | flops | bytes accessed | tf_op | source)
XLA Modules:
  0.0 202.0 jit_solution(14236669765198058881)
XLA Ops:
  6.5 0.7 all-gather.2.cloned.1.call-update
  7.3 84.3 %all-gather.2.cloned.1.call-done = bf16[6,1536,256]{2,1,0:T(8,128)(2,1)} async-done(((bf16[6,192,256]{2,1,0:T(8,128)(2,1)}), bf16[6,1536,256]{2,1,0:T(8,128)(2,1)}) %all-gather.2.cloned.1.call-update) | async-done | bytes 4718608 | tf_op jit(solution)/shard_map/all_gather | solution.py:33
  91.6 8.4 %fusion.34 = f32[512,256,1]{1,0,2:T(8,128)} fusion(bf16[6,512,1536]{2,1,0:T(8,128)(2,1)} %param.9, bf16[6,1536,256]{2,1,0:T(8,128)(2,1)} %all-gather.2.cloned.1.call-done), kind=kOutput, calls=%fused_computation.66 | convolution fusion | flops 2415919104 | bytes 14680064 | tf_op jit(solution)/shard_map/dot_general | solution.py:31
  100.1 0.7 fusion.22
  103.7 16.5 %reduce-scatter.2.cloned.1.call-done = f32[1,128,256]{2,1,0:T(8,128)} async-done(((f32[4,128,256]{2,1,0:T(8,128)}), f32[1,128,256]{2,1,0:T(8,128)}) %reduce-scatter.2.cloned.1.call-update) | async-done | bytes 131088 | tf_op jit(solution)/shard_map/reduce_scatter | solution.py:42
  120.2 6.8 %all_gather.16 = f32[4,128,256]{2,1,0:T(8,128)S(1)} all-gather(f32[1,128,256]{2,1,0:T(8,128)} %reduce-scatter.2.cloned.1.call-done), channel_id=1, replica_groups=mesh['row'=4,'col'=8] {'row'}, dimensions={0}, use_global_device_ids=true | all-gather | bytes 655360 | tf_op jit(solution)/shard_map/all_gather | solution.py:43
  127.2 5.9 %all_gather.17 = bf16[512,256]{0,1:T(8,128)(2,1)S(1)} all-gather(bf16[128,256]{0,1:T(8,128)(2,1)S(1)} %get-tuple-element.8), channel_id=1, replica_groups=mesh['row'=4,'col'=8] {'row'}, dimensions={0}, use_global_device_ids=true | all-gather | bytes 327680 | tf_op jit(solution)/shard_map/all_gather | solution.py:56
  133.1 1.5 collective-permute-start
  134.6 3.2 %collective-permute-start.1 = (bf16[512,256]{0,1:T(8,128)(2,1)S(1)}, bf16[512,256]{0,1:T(8,128)(2,1)S(1)}, u32[]{:S(2)}, u32[]{:S(2)}) collective-permute-start(bf16[512,256]{0,1:T(8,128)(2,1)S(1)} %all_gather.17), channel_id=1, source_target_pairs={{1,0},{2,1},{3,2},{4,3},{5,4},{6,5},{7,6},{0,7},{9,8},{10,9},{11,1... | collective-permute-start | bytes 786440 | tf_op jit(solution)/shard_map/ppermute | solution.py:19
  137.8 8.4 %collective-permute-done = bf16[512,256]{0,1:T(8,128)(2,1)S(1)} collective-permute-done((bf16[512,256]{0,1:T(8,128)(2,1)S(1)}, bf16[512,256]{0,1:T(8,128)(2,1)S(1)}, u32[]{:S(2)}, u32[]{:S(2)}) %collective-permute-start) | collective-permute-done | bytes 262176 | tf_op jit(solution)/shard_map/ppermute | solution.py:17
  146.2 2.2 %collective-permute-done.1 = bf16[512,256]{0,1:T(8,128)(2,1)S(1)} collective-permute-done((bf16[512,256]{0,1:T(8,128)(2,1)S(1)}, bf16[512,256]{0,1:T(8,128)(2,1)S(1)}, u32[]{:S(2)}, u32[]{:S(2)}) %collective-permute-start.1) | collective-permute-done | bytes 262176 | tf_op jit(solution)/shard_map/ppermute | solution.py:19
  148.8 0.6 gather_fusion
  149.4 0.5 fusion.32
  149.9 5.8 %all_gather.18 = bf16[512,256]{0,1:T(8,128)(2,1)S(1)} all-gather(bf16[128,256]{0,1:T(8,128)(2,1)S(1)} %get-tuple-element.10), channel_id=1, replica_groups=mesh['row'=4,'col'=8] {'row'}, dimensions={0}, use_global_device_ids=true | all-gather | bytes 327680 | tf_op jit(solution)/shard_map/all_gather | solution.py:56
  156.0 4.4 %collective-permute-start.3 = (bf16[512,256]{0,1:T(8,128)(2,1)S(1)}, bf16[512,256]{0,1:T(8,128)(2,1)S(1)}, u32[]{:S(2)}, u32[]{:S(2)}) collective-permute-start(bf16[512,256]{0,1:T(8,128)(2,1)S(1)} %all_gather.18), channel_id=1, source_target_pairs={{1,0},{2,1},{3,2},{4,3},{5,4},{6,5},{7,6},{0,7},{9,8},{10,9},{11,1... | collective-permute-start | bytes 786440 | tf_op jit(solution)/shard_map/ppermute | solution.py:19
  160.5 7.3 %collective-permute-done.2 = bf16[512,256]{0,1:T(8,128)(2,1)S(1)} collective-permute-done((bf16[512,256]{0,1:T(8,128)(2,1)S(1)}, bf16[512,256]{0,1:T(8,128)(2,1)S(1)}, u32[]{:S(2)}, u32[]{:S(2)}) %collective-permute-start.2) | collective-permute-done | bytes 262176 | tf_op jit(solution)/shard_map/ppermute | solution.py:17
  167.7 2.8 %collective-permute-done.3 = bf16[512,256]{0,1:T(8,128)(2,1)S(1)} collective-permute-done((bf16[512,256]{0,1:T(8,128)(2,1)S(1)}, bf16[512,256]{0,1:T(8,128)(2,1)S(1)}, u32[]{:S(2)}, u32[]{:S(2)}) %collective-permute-start.3) | collective-permute-done | bytes 262176 | tf_op jit(solution)/shard_map/ppermute | solution.py:19
  170.9 0.6 gather_fusion.1
  172.0 5.8 %all_gather.19 = bf16[512,256]{0,1:T(8,128)(2,1)S(1)} all-gather(bf16[128,256]{0,1:T(8,128)(2,1)S(1)} %get-tuple-element.12), channel_id=1, replica_groups=mesh['row'=4,'col'=8] {'row'}, dimensions={0}, use_global_device_ids=true | all-gather | bytes 327680 | tf_op jit(solution)/shard_map/all_gather | solution.py:56
  177.8 4.7 %collective-permute-start.5 = (bf16[512,256]{0,1:T(8,128)(2,1)S(1)}, bf16[512,256]{0,1:T(8,128)(2,1)S(1)}, u32[]{:S(2)}, u32[]{:S(2)}) collective-permute-start(bf16[512,256]{0,1:T(8,128)(2,1)S(1)} %all_gather.19), channel_id=1, source_target_pairs={{1,0},{2,1},{3,2},{4,3},{5,4},{6,5},{7,6},{0,7},{9,8},{10,9},{11,1... | collective-permute-start | bytes 786440 | tf_op jit(solution)/shard_map/ppermute | solution.py:19
  182.5 7.3 %collective-permute-done.4 = bf16[512,256]{0,1:T(8,128)(2,1)S(1)} collective-permute-done((bf16[512,256]{0,1:T(8,128)(2,1)S(1)}, bf16[512,256]{0,1:T(8,128)(2,1)S(1)}, u32[]{:S(2)}, u32[]{:S(2)}) %collective-permute-start.4) | collective-permute-done | bytes 262176 | tf_op jit(solution)/shard_map/ppermute | solution.py:17
  189.8 3.1 %collective-permute-done.5 = bf16[512,256]{0,1:T(8,128)(2,1)S(1)} collective-permute-done((bf16[512,256]{0,1:T(8,128)(2,1)S(1)}, bf16[512,256]{0,1:T(8,128)(2,1)S(1)}, u32[]{:S(2)}, u32[]{:S(2)}) %collective-permute-start.5) | collective-permute-done | bytes 262176 | tf_op jit(solution)/shard_map/ppermute | solution.py:19
  193.2 0.6 gather_fusion.2
  194.4 0.8 copy.37
  (29 shorter events, 2.8 us)
Async XLA Ops:
  6.5 142.9 %copy-start = (bf16[12,128,128]{2,1,0:T(8,128)(2,1)S(1)}, bf16[12,128,128]{2,1,0:T(8,128)(2,1)}, u32[]{:S(2)}) copy-start(bf16[12,128,128]{2,1,0:T(8,128)(2,1)} %param.14) | copy-start | bytes 1179652
  6.5 85.1 %all-gather.2.cloned.1.call-start = ((), (), s32[]{:S(2)}) async-start(), calls=%async_computation.1 | async-start | bytes 5308416 | tf_op jit(solution)/shard_map/all_gather | solution.py:33
  7.3 92.8 %copy-start.2 = (s32[32]{0:T(128)S(1)}, s32[32]{0:T(128)}, u32[]{:S(2)}) copy-start(s32[32]{0:T(128)} %param.12) | copy-start | bytes 388
  7.3 94.8 %copy-start.1 = (f32[1,128,256]{2,1,0:T(8,128)S(1)}, f32[1,128,256]{2,1,0:T(8,128)}, u32[]{:S(2)}) copy-start(f32[1,128,256]{2,1,0:T(8,128)} %param.11) | copy-start | bytes 393220
  7.3 96.2 %copy-start.3 = (s32[12,2]{0,1:T(2,128)S(1)}, s32[12,2]{0,1:T(2,128)}, u32[]{:S(2)}) copy-start(s32[12,2]{0,1:T(2,128)} %param.13) | copy-start | bytes 292
  7.3 112.9 %reduce-scatter.2.cloned.1.call-start = ((), (), s32[]{:S(2)}) async-start(), calls=%async_computation.2 | async-start | bytes 655360 | tf_op jit(solution)/shard_map/reduce_scatter | solution.py:42
  133.1 13.2 %collective-permute-start = (bf16[512,256]{0,1:T(8,128)(2,1)S(1)}, bf16[512,256]{0,1:T(8,128)(2,1)S(1)}, u32[]{:S(2)}, u32[]{:S(2)}) collective-permute-start(bf16[512,256]{0,1:T(8,128)(2,1)S(1)} %all_gather.17), channel_id=1, source_target_pairs={{0,1},{1,2},{2,3},{3,4},{4,5},{5,6},{6,7},{7,0},{8,9},{9,10},{10,1... | collective-permute-start | bytes 786440 | tf_op jit(solution)/shard_map/ppermute | solution.py:17
  134.6 13.9 %collective-permute-start.1 = (bf16[512,256]{0,1:T(8,128)(2,1)S(1)}, bf16[512,256]{0,1:T(8,128)(2,1)S(1)}, u32[]{:S(2)}, u32[]{:S(2)}) collective-permute-start(bf16[512,256]{0,1:T(8,128)(2,1)S(1)} %all_gather.17), channel_id=1, source_target_pairs={{1,0},{2,1},{3,2},{4,3},{5,4},{6,5},{7,6},{0,7},{9,8},{10,9},{11,1... | collective-permute-start | bytes 786440 | tf_op jit(solution)/shard_map/ppermute | solution.py:19
  155.7 12.0 %collective-permute-start.2 = (bf16[512,256]{0,1:T(8,128)(2,1)S(1)}, bf16[512,256]{0,1:T(8,128)(2,1)S(1)}, u32[]{:S(2)}, u32[]{:S(2)}) collective-permute-start(bf16[512,256]{0,1:T(8,128)(2,1)S(1)} %all_gather.18), channel_id=1, source_target_pairs={{0,1},{1,2},{2,3},{3,4},{4,5},{5,6},{6,7},{7,0},{8,9},{9,10},{10,1... | collective-permute-start | bytes 786440 | tf_op jit(solution)/shard_map/ppermute | solution.py:17
  156.0 14.5 %collective-permute-start.3 = (bf16[512,256]{0,1:T(8,128)(2,1)S(1)}, bf16[512,256]{0,1:T(8,128)(2,1)S(1)}, u32[]{:S(2)}, u32[]{:S(2)}) collective-permute-start(bf16[512,256]{0,1:T(8,128)(2,1)S(1)} %all_gather.18), channel_id=1, source_target_pairs={{1,0},{2,1},{3,2},{4,3},{5,4},{6,5},{7,6},{0,7},{9,8},{10,9},{11,1... | collective-permute-start | bytes 786440 | tf_op jit(solution)/shard_map/ppermute | solution.py:19
  177.8 12.0 %collective-permute-start.4 = (bf16[512,256]{0,1:T(8,128)(2,1)S(1)}, bf16[512,256]{0,1:T(8,128)(2,1)S(1)}, u32[]{:S(2)}, u32[]{:S(2)}) collective-permute-start(bf16[512,256]{0,1:T(8,128)(2,1)S(1)} %all_gather.19), channel_id=1, source_target_pairs={{0,1},{1,2},{2,3},{3,4},{4,5},{5,6},{6,7},{7,0},{8,9},{9,10},{10,1... | collective-permute-start | bytes 786440 | tf_op jit(solution)/shard_map/ppermute | solution.py:17
  177.8 15.1 %collective-permute-start.5 = (bf16[512,256]{0,1:T(8,128)(2,1)S(1)}, bf16[512,256]{0,1:T(8,128)(2,1)S(1)}, u32[]{:S(2)}, u32[]{:S(2)}) collective-permute-start(bf16[512,256]{0,1:T(8,128)(2,1)S(1)} %all_gather.19), channel_id=1, source_target_pairs={{1,0},{2,1},{3,2},{4,3},{5,4},{6,5},{7,6},{0,7},{9,8},{10,9},{11,1... | collective-permute-start | bytes 786440 | tf_op jit(solution)/shard_map/ppermute | solution.py:19
Sparse Core Ops, SparseCore 0:
  9.5 82.0 all-gather.1
  100.2 20.0 reduce-scatter.1
where the time goes:
time: 202 us
  waiting for transfers between devices  133 us (66%)
  blocking collectives  24.3 us (12%)
  between operations  16.2 us (8%)
  starting transfers between devices  14.2 us (7%)
  matrix products  10 us (5%)
  local copies, waits for them, and re-layouts  3.57 us (2%)
    all_gather x1, waiting for transfers between devices, per_device(): lax.all_gather(history, 'col', axis=1, tiled=True)  84.3 us
    ppermute x3, waiting for transfers between devices, with_halo(): lax.ppermute(tail, axis, [(i, (i + 1) % count) for i in range(count)])  22.9 us
    all_gather x3, blocking collectives, per_device(): block_part = lax.all_gather(rounded, 'row', axis=0, tiled=True)  17.5 us
    reduce_scatter x1, waiting for transfers between devices, per_device(): block_sum = lax.psum_scatter(blocks, 'row', scatter_dimension=0, tiled=True)  16.5 us
    ppermute x3, starting transfers between devices, with_halo(): lax.ppermute(head, axis, [((i + 1) % count, i) for i in range(count)])  12.4 us
    dot_general x1, matrix products, per_device(): lax.dot_general(kernels, lax.all_gather(history, 'col', axis=1, tiled=Tru...  8.41 us
    ppermute x3, waiting for transfers between devices, with_halo(): lax.ppermute(head, axis, [((i + 1) % count, i) for i in range(count)])  8.1 us
    all_gather x1, blocking collectives, per_device(): everyone = lax.all_gather(block_sum, 'row', axis=0, tiled=True)  6.78 us
  transfers between devices with their start and end apart: 8, of which 8 were waited for; matrix products, arithmetic and copies ran while one was open for 1% of the time, Pallas kernels for 0%

commit v1 on v0

--- a/solution.py
+++ b/solution.py
@@ -5,6 +5,23 @@
 
 SWEEPS = 3
 damping = 0.7
+
+
+def in_order(tiles, dim):
+    dims = list(tiles.shape[1:])
+    dims[dim] *= tiles.shape[0]
+    return jnp.moveaxis(tiles, 0, dim).reshape(dims)
+
+
+def gather_around(x, axis, dim):
+    devices = lax.axis_size(axis)
+    right = [(i, (i + 1) % devices) for i in range(devices)]
+    parts = [x]
+    while len(parts) < devices:
+        parts.append(lax.ppermute(parts[-1], axis, right))
+    index = lax.axis_index(axis)
+    parts = jnp.stack(parts)[(index - jnp.arange(devices)) % devices]
+    return in_order(parts, dim)
 
 
 def with_halo(cells, sides, width):
@@ -30,7 +47,7 @@
     cluster = incident.shape[1]
     retarded = lax.dot_general(
         kernels,
-        lax.all_gather(history, "col", axis=1, tiled=True),
+        gather_around(history, "col", 1),
         (((0, 2), (0, 1)), ((), ())),
         preferred_element_type=jnp.float32,
     )

time: 202 us -> 231 us (1.14)
  local copies, waits for them, and re-layouts: 3.57 us -> 20.5 us
  waiting for transfers between devices: 133 us -> 147 us
  matrix products: 10 us -> 6.92 us
    ppermute x0 -> x7, waiting for transfers between devices: none -> 99.7 us  [gather_around(): parts.append(lax.ppermute(parts[-1], axis, right))]
    all_gather x1 -> x0, waiting for transfers between devices: 84.3 us -> none  [per_device(): lax.all_gather(history, 'col', axis=1, tiled=True)]
    ppermute x3, waiting for transfers between devices: 8.1 us -> 23.3 us  [with_halo(): lax.ppermute(head, axis, [((i + 1) % count, i) for i in range(count)])]
    ppermute x3, waiting for transfers between devices: 22.9 us -> 9.98 us  [with_halo(): lax.ppermute(tail, axis, [(i, (i + 1) % count) for i in range(count)])]
    unnamed x10 -> x17, local copies, waits for them, and re-layouts: 0.19 us -> 7.29 us
    gather x0 -> x1, local copies, waits for them, and re-layouts: none -> 5.36 us  [gather_around(): parts = jnp.stack(parts)[(index - jnp.arange(devices)) % devices]]
    dot_general x1, matrix products: 8.41 us -> 5.31 us  [per_device(): lax.dot_general(kernels, gather_around(history, 'col', 1), (((0, 2), (0,...]
    ppermute x0 -> x7, starting transfers between devices: none -> 2.98 us  [gather_around(): parts.append(lax.ppermute(parts[-1], axis, right))]
  transfers between devices with their start and end apart: 8 -> 14, of which waited for: 8 -> 14; matrix products, arithmetic and copies ran while one was open for 1% -> 4% of each run, Pallas kernels for 0% -> 0%
where the time goes in v1:
time: 231 us; the launch traced here: 230 us
  waiting for transfers between devices  147 us (64%)
  blocking collectives  24.3 us (11%)
  local copies, waits for them, and re-layouts  20.5 us (9%)
  between operations  16.2 us (7%)
  starting transfers between devices  13.9 us (6%)
  matrix products  6.92 us (3%)
    ppermute x7, waiting for transfers between devices, gather_around(): parts.append(lax.ppermute(parts[-1], axis, right))  99.7 us
    ppermute x3, waiting for transfers between devices, with_halo(): lax.ppermute(head, axis, [((i + 1) % count, i) for i in range(count)])  23.3 us
    all_gather x3, blocking collectives, per_device(): block_part = lax.all_gather(rounded, 'row', axis=0, tiled=True)  17.5 us
    reduce_scatter x1, waiting for transfers between devices, per_device(): block_sum = lax.psum_scatter(blocks, 'row', scatter_dimension=0, tiled=True)  14.3 us
    ppermute x3, starting transfers between devices, with_halo(): lax.ppermute(head, axis, [((i + 1) % count, i) for i in range(count)])  10.9 us
    ppermute x3, waiting for transfers between devices, with_halo(): lax.ppermute(tail, axis, [(i, (i + 1) % count) for i in range(count)])  9.98 us
    unnamed x17, local copies, waits for them, and re-layouts  7.29 us
    all_gather x1, blocking collectives, per_device(): everyone = lax.all_gather(block_sum, 'row', axis=0, tiled=True)  6.8 us
  transfers between devices with their start and end apart: 14, of which 14 were waited for; matrix products, arithmetic and copies ran while one was open for 4% of the time, Pallas kernels for 0%

profile of v1, /device:TPU:0, one launch (start us, length us, event | category | flops | bytes accessed | tf_op | source)
XLA Modules:
  0.0 230.3 jit_solution(4243331254793581546)
XLA Ops:
  6.5 3.0 %collective-permute-start = (bf16[6,192,256]{2,1,0:T(8,128)(2,1)}, bf16[6,192,256]{2,1,0:T(8,128)(2,1)S(1)}, u32[]{:S(2)}, u32[]{:S(2)}) collective-permute-start(bf16[6,192,256]{2,1,0:T(8,128)(2,1)} %param.10), channel_id=1, source_target_pairs={{0,1},{1,2},{2,3},{3,4},{4,5},{5,6},{6,7},{7,0},{8,9},{9,10},{10,1... | collective-permute-start | bytes 1769480 | tf_op jit(solution)/shard_map/ppermute | solution.py:21
  9.5 16.6 %collective-permute-done = bf16[6,192,256]{2,1,0:T(8,128)(2,1)S(1)} collective-permute-done((bf16[6,192,256]{2,1,0:T(8,128)(2,1)}, bf16[6,192,256]{2,1,0:T(8,128)(2,1)S(1)}, u32[]{:S(2)}, u32[]{:S(2)}) %collective-permute-start) | collective-permute-done | bytes 589856 | tf_op jit(solution)/shard_map/ppermute | solution.py:21
  26.1 17.2 %collective-permute-done.1 = bf16[6,192,256]{2,1,0:T(8,128)(2,1)S(1)} collective-permute-done((bf16[6,192,256]{2,1,0:T(8,128)(2,1)S(1)}, bf16[6,192,256]{2,1,0:T(8,128)(2,1)S(1)}, u32[]{:S(2)}, u32[]{:S(2)}) %collective-permute-start.1) | collective-permute-done | bytes 589856 | tf_op jit(solution)/shard_map/ppermute | solution.py:21
  43.3 16.3 %collective-permute-done.2 = bf16[6,192,256]{2,1,0:T(8,128)(2,1)S(1)} collective-permute-done((bf16[6,192,256]{2,1,0:T(8,128)(2,1)S(1)}, bf16[6,192,256]{2,1,0:T(8,128)(2,1)S(1)}, u32[]{:S(2)}, u32[]{:S(2)}) %collective-permute-start.2) | collective-permute-done | bytes 589856 | tf_op jit(solution)/shard_map/ppermute | solution.py:21
  59.6 15.5 %collective-permute-done.3 = bf16[6,192,256]{2,1,0:T(8,128)(2,1)S(1)} collective-permute-done((bf16[6,192,256]{2,1,0:T(8,128)(2,1)S(1)}, bf16[6,192,256]{2,1,0:T(8,128)(2,1)S(1)}, u32[]{:S(2)}, u32[]{:S(2)}) %collective-permute-start.3) | collective-permute-done | bytes 589856 | tf_op jit(solution)/shard_map/ppermute | solution.py:21
  77.0 12.7 %collective-permute-done.4 = bf16[6,192,256]{2,1,0:T(8,128)(2,1)S(1)} collective-permute-done((bf16[6,192,256]{2,1,0:T(8,128)(2,1)S(1)}, bf16[6,192,256]{2,1,0:T(8,128)(2,1)S(1)}, u32[]{:S(2)}, u32[]{:S(2)}) %collective-permute-start.4) | collective-permute-done | bytes 589856 | tf_op jit(solution)/shard_map/ppermute | solution.py:21
  92.3 11.2 %collective-permute-done.5 = bf16[6,192,256]{2,1,0:T(8,128)(2,1)S(1)} collective-permute-done((bf16[6,192,256]{2,1,0:T(8,128)(2,1)S(1)}, bf16[6,192,256]{2,1,0:T(8,128)(2,1)S(1)}, u32[]{:S(2)}, u32[]{:S(2)}) %collective-permute-start.5) | collective-permute-done | bytes 589856 | tf_op jit(solution)/shard_map/ppermute | solution.py:21
  106.0 10.3 %collective-permute-done.6 = bf16[6,192,256]{2,1,0:T(8,128)(2,1)S(1)} collective-permute-done((bf16[6,192,256]{2,1,0:T(8,128)(2,1)S(1)}, bf16[6,192,256]{2,1,0:T(8,128)(2,1)S(1)}, u32[]{:S(2)}, u32[]{:S(2)}) %collective-permute-start.6) | collective-permute-done | bytes 589856 | tf_op jit(solution)/shard_map/ppermute | solution.py:21
  117.2 5.4 %gather_fusion = bf16[8,6,192,256]{3,2,1,0:T(8,128)(2,1)} fusion(bf16[8,6,192,256]{3,2,1,0:T(8,128)(2,1)} %bitcast_dynamic-update-slice_fusion, s32[1024]{0:T(1024)S(1)} %pad_clamp_fusion.1), kind=kCustom, calls=%fused_computation.3 | custom fusion | bytes 9437216 | tf_op jit(solution)/shard_map/gather | solution.py:23
  122.6 2.6 %copy.44 = bf16[6,8,192,256]{3,2,1,0:T(8,128)(2,1)S(1)} copy(bf16[6,8,192,256]{3,2,0,1:T(8,128)(2,1)} %bitcast.86) | data formatting | bytes 9437184 | tf_op jit(solution)/shard_map/transpose | solution.py:13
  125.3 5.3 %convolution_bitcast_fusion = f32[512,256]{0,1:T(8,128)S(1)} fusion(bf16[6,1536,256]{2,1,0:T(8,128)(2,1)S(1)} %bitcast.87, bf16[6,512,1536]{2,1,0:T(8,128)(2,1)} %param.9), kind=kOutput, calls=%fused_computation.4 | convolution fusion | flops 2415919104 | bytes 14680064 | tf_op jit(solution)/shard_map/dot_general | solution.py:48
  135.3 14.3 %reduce-scatter.2.cloned.1.call-done = f32[1,128,256]{2,1,0:T(8,128)} async-done(((f32[4,128,256]{2,1,0:T(8,128)}), f32[1,128,256]{2,1,0:T(8,128)}) %reduce-scatter.2.cloned.1.call-update) | async-done | bytes 131088 | tf_op jit(solution)/shard_map/reduce_scatter | solution.py:59
  149.6 6.8 %all_gather.12 = f32[4,128,256]{2,1,0:T(8,128)S(1)} all-gather(f32[1,128,256]{2,1,0:T(8,128)} %reduce-scatter.2.cloned.1.call-done), channel_id=1, replica_groups=mesh['row'=4,'col'=8] {'row'}, dimensions={0}, use_global_device_ids=true | all-gather | bytes 655360 | tf_op jit(solution)/shard_map/all_gather | solution.py:60
  156.5 5.9 %all_gather.13 = bf16[512,256]{0,1:T(8,128)(2,1)S(1)} all-gather(bf16[128,256]{0,1:T(8,128)(2,1)S(1)} %get-tuple-element.8), channel_id=1, replica_groups=mesh['row'=4,'col'=8] {'row'}, dimensions={0}, use_global_device_ids=true | all-gather | bytes 327680 | tf_op jit(solution)/shard_map/all_gather | solution.py:73
  162.4 4.2 %collective-permute-start.8 = (bf16[512,256]{0,1:T(8,128)(2,1)S(1)}, bf16[512,256]{0,1:T(8,128)(2,1)S(1)}, u32[]{:S(2)}, u32[]{:S(2)}) collective-permute-start(bf16[512,256]{0,1:T(8,128)(2,1)S(1)} %all_gather.13), channel_id=1, source_target_pairs={{1,0},{2,1},{3,2},{4,3},{5,4},{6,5},{7,6},{0,7},{9,8},{10,9},{11,1... | collective-permute-start | bytes 786440 | tf_op jit(solution)/shard_map/ppermute | solution.py:36
  166.7 6.0 %collective-permute-done.8 = bf16[512,256]{0,1:T(8,128)(2,1)S(1)} collective-permute-done((bf16[512,256]{0,1:T(8,128)(2,1)S(1)}, bf16[512,256]{0,1:T(8,128)(2,1)S(1)}, u32[]{:S(2)}, u32[]{:S(2)}) %collective-permute-start.8) | collective-permute-done | bytes 262176 | tf_op jit(solution)/shard_map/ppermute | solution.py:36
  172.7 4.9 %collective-permute-done.7 = bf16[512,256]{0,1:T(8,128)(2,1)S(1)} collective-permute-done((bf16[512,256]{0,1:T(8,128)(2,1)S(1)}, bf16[512,256]{0,1:T(8,128)(2,1)S(1)}, u32[]{:S(2)}, u32[]{:S(2)}) %collective-permute-start.7) | collective-permute-done | bytes 262176 | tf_op jit(solution)/shard_map/ppermute | solution.py:34
  179.1 5.8 %all_gather.14 = bf16[512,256]{0,1:T(8,128)(2,1)S(1)} all-gather(bf16[128,256]{0,1:T(8,128)(2,1)S(1)} %get-tuple-element.10), channel_id=1, replica_groups=mesh['row'=4,'col'=8] {'row'}, dimensions={0}, use_global_device_ids=true | all-gather | bytes 327680 | tf_op jit(solution)/shard_map/all_gather | solution.py:73
  184.9 3.5 %collective-permute-start.10 = (bf16[512,256]{0,1:T(8,128)(2,1)S(1)}, bf16[512,256]{0,1:T(8,128)(2,1)S(1)}, u32[]{:S(2)}, u32[]{:S(2)}) collective-permute-start(bf16[512,256]{0,1:T(8,128)(2,1)S(1)} %all_gather.14), channel_id=1, source_target_pairs={{1,0},{2,1},{3,2},{4,3},{5,4},{6,5},{7,6},{0,7},{9,8},{10,9},{11,1... | collective-permute-start | bytes 786440 | tf_op jit(solution)/shard_map/ppermute | solution.py:36
  188.4 6.1 %collective-permute-done.10 = bf16[512,256]{0,1:T(8,128)(2,1)S(1)} collective-permute-done((bf16[512,256]{0,1:T(8,128)(2,1)S(1)}, bf16[512,256]{0,1:T(8,128)(2,1)S(1)}, u32[]{:S(2)}, u32[]{:S(2)}) %collective-permute-start.10) | collective-permute-done | bytes 262176 | tf_op jit(solution)/shard_map/ppermute | solution.py:36
  194.5 4.9 %collective-permute-done.9 = bf16[512,256]{0,1:T(8,128)(2,1)S(1)} collective-permute-done((bf16[512,256]{0,1:T(8,128)(2,1)S(1)}, bf16[512,256]{0,1:T(8,128)(2,1)S(1)}, u32[]{:S(2)}, u32[]{:S(2)}) %collective-permute-start.9) | collective-permute-done | bytes 262176 | tf_op jit(solution)/shard_map/ppermute | solution.py:34
  200.8 5.8 %all_gather.15 = bf16[512,256]{0,1:T(8,128)(2,1)S(1)} all-gather(bf16[128,256]{0,1:T(8,128)(2,1)S(1)} %get-tuple-element.12), channel_id=1, replica_groups=mesh['row'=4,'col'=8] {'row'}, dimensions={0}, use_global_device_ids=true | all-gather | bytes 327680 | tf_op jit(solution)/shard_map/all_gather | solution.py:73
  206.7 3.2 %collective-permute-start.12 = (bf16[512,256]{0,1:T(8,128)(2,1)S(1)}, bf16[512,256]{0,1:T(8,128)(2,1)S(1)}, u32[]{:S(2)}, u32[]{:S(2)}) collective-permute-start(bf16[512,256]{0,1:T(8,128)(2,1)S(1)} %all_gather.15), channel_id=1, source_target_pairs={{1,0},{2,1},{3,2},{4,3},{5,4},{6,5},{7,6},{0,7},{9,8},{10,9},{11,1... | collective-permute-start | bytes 786440 | tf_op jit(solution)/shard_map/ppermute | solution.py:36
  209.9 11.2 %collective-permute-done.12 = bf16[512,256]{0,1:T(8,128)(2,1)S(1)} collective-permute-done((bf16[512,256]{0,1:T(8,128)(2,1)S(1)}, bf16[512,256]{0,1:T(8,128)(2,1)S(1)}, u32[]{:S(2)}, u32[]{:S(2)}) %collective-permute-start.12) | collective-permute-done | bytes 262176 | tf_op jit(solution)/shard_map/ppermute | solution.py:36
  (53 shorter events, 15.5 us)
Async XLA Ops:
  6.5 172.0 %copy-start = (bf16[12,128,128]{2,1,0:T(8,128)(2,1)S(1)}, bf16[12,128,128]{2,1,0:T(8,128)(2,1)}, u32[]{:S(2)}) copy-start(bf16[12,128,128]{2,1,0:T(8,128)(2,1)} %param.14) | copy-start | bytes 1179652
  6.5 143.0 %reduce-scatter.2.cloned.1.call-start = ((), (), s32[]{:S(2)}) async-start(), calls=%async_computation.1 | async-start | bytes 655360 | tf_op jit(solution)/shard_map/reduce_scatter | solution.py:59
  6.5 19.5 %collective-permute-start = (bf16[6,192,256]{2,1,0:T(8,128)(2,1)}, bf16[6,192,256]{2,1,0:T(8,128)(2,1)S(1)}, u32[]{:S(2)}, u32[]{:S(2)}) collective-permute-start(bf16[6,192,256]{2,1,0:T(8,128)(2,1)} %param.10), channel_id=1, source_target_pairs={{0,1},{1,2},{2,3},{3,4},{4,5},{5,6},{6,7},{7,0},{8,9},{9,10},{10,1... | collective-permute-start | bytes 1769480 | tf_op jit(solution)/shard_map/ppermute | solution.py:21
  26.1 17.2 %collective-permute-start.1 = (bf16[6,192,256]{2,1,0:T(8,128)(2,1)S(1)}, bf16[6,192,256]{2,1,0:T(8,128)(2,1)S(1)}, u32[]{:S(2)}, u32[]{:S(2)}) collective-permute-start(bf16[6,192,256]{2,1,0:T(8,128)(2,1)S(1)} %collective-permute-done), channel_id=1, source_target_pairs={{0,1},{1,2},{2,3},{3,4},{4,5},{5,6},{6,7},{7,0},{8,9},{9,10},{10,1... | collective-permute-start | bytes 1769480 | tf_op jit(solution)/shard_map/ppermute | solution.py:21
  43.3 16.3 %collective-permute-start.2 = (bf16[6,192,256]{2,1,0:T(8,128)(2,1)S(1)}, bf16[6,192,256]{2,1,0:T(8,128)(2,1)S(1)}, u32[]{:S(2)}, u32[]{:S(2)}) collective-permute-start(bf16[6,192,256]{2,1,0:T(8,128)(2,1)S(1)} %collective-permute-done.1), channel_id=1, source_target_pairs={{0,1},{1,2},{2,3},{3,4},{4,5},{5,6},{6,7},{7,0},{8,9},{9,10},{10,1... | collective-permute-start | bytes 1769480 | tf_op jit(solution)/shard_map/ppermute | solution.py:21
  59.6 15.5 %collective-permute-start.3 = (bf16[6,192,256]{2,1,0:T(8,128)(2,1)S(1)}, bf16[6,192,256]{2,1,0:T(8,128)(2,1)S(1)}, u32[]{:S(2)}, u32[]{:S(2)}) collective-permute-start(bf16[6,192,256]{2,1,0:T(8,128)(2,1)S(1)} %collective-permute-done.2), channel_id=1, source_target_pairs={{0,1},{1,2},{2,3},{3,4},{4,5},{5,6},{6,7},{7,0},{8,9},{9,10},{10,1... | collective-permute-start | bytes 1769480 | tf_op jit(solution)/shard_map/ppermute | solution.py:21
  75.1 14.6 %collective-permute-start.4 = (bf16[6,192,256]{2,1,0:T(8,128)(2,1)S(1)}, bf16[6,192,256]{2,1,0:T(8,128)(2,1)S(1)}, u32[]{:S(2)}, u32[]{:S(2)}) collective-permute-start(bf16[6,192,256]{2,1,0:T(8,128)(2,1)S(1)} %collective-permute-done.3), channel_id=1, source_target_pairs={{0,1},{1,2},{2,3},{3,4},{4,5},{5,6},{6,7},{7,0},{8,9},{9,10},{10,1... | collective-permute-start | bytes 1769480 | tf_op jit(solution)/shard_map/ppermute | solution.py:21
  89.7 13.8 %collective-permute-start.5 = (bf16[6,192,256]{2,1,0:T(8,128)(2,1)S(1)}, bf16[6,192,256]{2,1,0:T(8,128)(2,1)S(1)}, u32[]{:S(2)}, u32[]{:S(2)}) collective-permute-start(bf16[6,192,256]{2,1,0:T(8,128)(2,1)S(1)} %collective-permute-done.4), channel_id=1, source_target_pairs={{0,1},{1,2},{2,3},{3,4},{4,5},{5,6},{6,7},{7,0},{8,9},{9,10},{10,1... | collective-permute-start | bytes 1769480 | tf_op jit(solution)/shard_map/ppermute | solution.py:21
  103.5 12.9 %collective-permute-start.6 = (bf16[6,192,256]{2,1,0:T(8,128)(2,1)S(1)}, bf16[6,192,256]{2,1,0:T(8,128)(2,1)S(1)}, u32[]{:S(2)}, u32[]{:S(2)}) collective-permute-start(bf16[6,192,256]{2,1,0:T(8,128)(2,1)S(1)} %collective-permute-done.5), channel_id=1, source_target_pairs={{0,1},{1,2},{2,3},{3,4},{4,5},{5,6},{6,7},{7,0},{8,9},{9,10},{10,1... | collective-permute-start | bytes 1769480 | tf_op jit(solution)/shard_map/ppermute | solution.py:21
  125.3 6.4 %copy-start.2 = (s32[32]{0:T(128)S(1)}, s32[32]{0:T(128)}, u32[]{:S(2)}) copy-start(s32[32]{0:T(128)} %param.12) | copy-start | bytes 388
  125.3 8.4 %copy-start.1 = (f32[1,128,256]{2,1,0:T(8,128)S(1)}, f32[1,128,256]{2,1,0:T(8,128)}, u32[]{:S(2)}) copy-start(f32[1,128,256]{2,1,0:T(8,128)} %param.11) | copy-start | bytes 393220
  125.3 9.8 %copy-start.3 = (s32[12,2]{0,1:T(2,128)S(1)}, s32[12,2]{0,1:T(2,128)}, u32[]{:S(2)}) copy-start(s32[12,2]{0,1:T(2,128)} %param.13) | copy-start | bytes 292
  162.4 10.3 %collective-permute-start.8 = (bf16[512,256]{0,1:T(8,128)(2,1)S(1)}, bf16[512,256]{0,1:T(8,128)(2,1)S(1)}, u32[]{:S(2)}, u32[]{:S(2)}) collective-permute-start(bf16[512,256]{0,1:T(8,128)(2,1)S(1)} %all_gather.13), channel_id=1, source_target_pairs={{1,0},{2,1},{3,2},{4,3},{5,4},{6,5},{7,6},{0,7},{9,8},{10,9},{11,1... | collective-permute-start | bytes 786440 | tf_op jit(solution)/shard_map/ppermute | solution.py:36
  166.7 11.0 %collective-permute-start.7 = (bf16[512,256]{0,1:T(8,128)(2,1)S(1)}, bf16[512,256]{0,1:T(8,128)(2,1)S(1)}, u32[]{:S(2)}, u32[]{:S(2)}) collective-permute-start(bf16[512,256]{0,1:T(8,128)(2,1)S(1)} %all_gather.13), channel_id=1, source_target_pairs={{0,1},{1,2},{2,3},{3,4},{4,5},{5,6},{6,7},{7,0},{8,9},{9,10},{10,1... | collective-permute-start | bytes 786440 | tf_op jit(solution)/shard_map/ppermute | solution.py:34
  184.9 9.5 %collective-permute-start.10 = (bf16[512,256]{0,1:T(8,128)(2,1)S(1)}, bf16[512,256]{0,1:T(8,128)(2,1)S(1)}, u32[]{:S(2)}, u32[]{:S(2)}) collective-permute-start(bf16[512,256]{0,1:T(8,128)(2,1)S(1)} %all_gather.14), channel_id=1, source_target_pairs={{1,0},{2,1},{3,2},{4,3},{5,4},{6,5},{7,6},{0,7},{9,8},{10,9},{11,1... | collective-permute-start | bytes 786440 | tf_op jit(solution)/shard_map/ppermute | solution.py:36
  188.4 11.0 %collective-permute-start.9 = (bf16[512,256]{0,1:T(8,128)(2,1)S(1)}, bf16[512,256]{0,1:T(8,128)(2,1)S(1)}, u32[]{:S(2)}, u32[]{:S(2)}) collective-permute-start(bf16[512,256]{0,1:T(8,128)(2,1)S(1)} %all_gather.14), channel_id=1, source_target_pairs={{0,1},{1,2},{2,3},{3,4},{4,5},{5,6},{6,7},{7,0},{8,9},{9,10},{10,1... | collective-permute-start | bytes 786440 | tf_op jit(solution)/shard_map/ppermute | solution.py:34
  206.7 14.4 %collective-permute-start.12 = (bf16[512,256]{0,1:T(8,128)(2,1)S(1)}, bf16[512,256]{0,1:T(8,128)(2,1)S(1)}, u32[]{:S(2)}, u32[]{:S(2)}) collective-permute-start(bf16[512,256]{0,1:T(8,128)(2,1)S(1)} %all_gather.15), channel_id=1, source_target_pairs={{1,0},{2,1},{3,2},{4,3},{5,4},{6,5},{7,6},{0,7},{9,8},{10,9},{11,1... | collective-permute-start | bytes 786440 | tf_op jit(solution)/shard_map/ppermute | solution.py:36
  209.9 11.4 %collective-permute-start.11 = (bf16[512,256]{0,1:T(8,128)(2,1)S(1)}, bf16[512,256]{0,1:T(8,128)(2,1)S(1)}, u32[]{:S(2)}, u32[]{:S(2)}) collective-permute-start(bf16[512,256]{0,1:T(8,128)(2,1)S(1)} %all_gather.15), channel_id=1, source_target_pairs={{0,1},{1,2},{2,3},{3,4},{4,5},{5,6},{6,7},{7,0},{8,9},{9,10},{10,1... | collective-permute-start | bytes 786440 | tf_op jit(solution)/shard_map/ppermute | solution.py:34
Sparse Core Ops, SparseCore 0:
  131.8 17.7 reduce-scatter.1
